TPU v7x, 1024 devices: a whole 4x4x32 slice. The times are simulated.
1024 devices in a mesh: ctx: 128 (over z_lo, y, x), head: 8 (over z_hi, core).
Axes of the slice: x: 4, y: 4, z: 32 (z_hi: 4, z_lo: 8; z = z_hi * 8 + z_lo), core: 2. Of those that a mesh axis runs over, the one named last changes fastest.
Arguments:
- queries: bfloat16 [32768, 8192], P('ctx', 'head'), may hold values from -120 to 120, as said below
- keys: bfloat16 [32768, 1024], P(('ctx', 'head')), may hold values from -6 to 6
- values: bfloat16 [32768, 1024], P(('ctx', 'head')), may hold values from -6 to 6
- doc_ids: int32 [32768], replicated, may hold values from 0 to 255, never falling along the last dimension, each value on 1 to 512 neighbouring positions
- output_gradient: bfloat16 [32768, 8192], P('ctx', 'head'), may hold values from -6 to 6
Outputs:
- attended: bfloat16 [32768, 8192], P('ctx', 'head')
- query_grad: bfloat16 [32768, 8192], P('ctx', 'head')
- key_grad: bfloat16 [32768, 1024], P(('ctx', 'head'))
- value_grad: bfloat16 [32768, 1024], P(('ctx', 'head'))
Inputs may be any that keep to these rules, and one draw needn't show every extreme that they name: `queries`: queries lie within -120 to 120 (up to 20 times a key entry), so scores may exceed 200.
All inputs are finite; a program needn't handle non-finite values.
Results may differ from a plain program's by a relative error of at most 0.012.
The roundings to bfloat16 on the way count: a program that leaves them out, or rounds other values in their place, can miss the bound.
Values may be sent and summed in bfloat16 or wider, within the bound.
A program may use at most 32 MiB of HBM per device.

v0:
```python
import jax
import jax.numpy as jnp
from jax import lax
from jax.sharding import PartitionSpec as P

HEAD_SIZE = 128
SPAN = 2


masked_value = -1e30


def shifted(x, axis, by):
    size = lax.axis_size(axis)
    pairs = [(i, i + by) for i in range(size) if 0 <= i + by < size]
    return lax.ppermute(x, axis, pairs)


def doc_visible(doc_ids, query_start, key_start, query_count, key_count, margin_rows):
    padded = jnp.concatenate(
        [jnp.full((margin_rows,), -1, jnp.int32), doc_ids, jnp.full((margin_rows,), -2, jnp.int32)]
    )
    query_docs = lax.dynamic_slice_in_dim(padded, query_start + margin_rows, query_count, 0)
    key_docs = lax.dynamic_slice_in_dim(padded, key_start + margin_rows, key_count, 0)
    query_places = query_start + jnp.arange(query_count, dtype=jnp.int32)
    key_places = key_start + jnp.arange(key_count, dtype=jnp.int32)
    return (key_places[None, :] <= query_places[:, None]) & (
        key_docs[None, :] == query_docs[:, None]
    )


def pair_scores(query_pair, key_block, visible):
    scores = jnp.einsum(
        "tgd,wd->gtw", query_pair, key_block, preferred_element_type=jnp.float32
    ) * HEAD_SIZE ** (-0.5)
    return jnp.where(visible[None], scores, masked_value)


def forward_heads(query3, key_window, value_window, visible):
    row_total = query3.shape[0]
    head_count = query3.shape[1]

    def forward_step_pair(carry, pair_index):
        attended_all, log_all = carry
        first = 2 * pair_index
        query_pair = lax.dynamic_slice_in_dim(query3, first, 2, 1)
        scores = pair_scores(query_pair, key_window, visible)
        row_max = jnp.max(scores, axis=2, keepdims=True)
        row_sum = jnp.sum(jnp.exp(scores - row_max), axis=2, keepdims=True)
        log_totals = row_max + jnp.log(row_sum)
        weights = jnp.where(visible[None], jnp.exp(scores - log_totals), 0.0).astype(jnp.bfloat16)
        attended = jnp.einsum(
            "gtw,wd->tgd", weights, value_window, preferred_element_type=jnp.float32
        ).astype(jnp.bfloat16)
        attended_all = lax.dynamic_update_slice_in_dim(attended_all, attended, first, 1)
        log_all = lax.dynamic_update_slice_in_dim(log_all, log_totals[:, :, 0], first, 0)
        return ((attended_all, log_all), None)

    offset_position = (
        jnp.zeros((row_total, head_count, HEAD_SIZE), jnp.bfloat16),
        jnp.zeros((head_count, row_total), jnp.float32),
    )
    (attended_all, log_all), unused = lax.scan(
        forward_step_pair, offset_position, jnp.arange(head_count // 2, dtype=jnp.int32)
    )
    return (attended_all, log_all)


def backward_heads(query3, grad3, log_all, deltas, key_window, value_window, visible):
    row_total = query3.shape[0]
    head_count = query3.shape[1]
    visible_span = key_window.shape[0]
    kv_heads = key_window.shape[1] // HEAD_SIZE

    def backward_step_pair(carry, pair_index):
        query_acc, key_acc, value_acc = carry
        first = 2 * pair_index
        query_pair = lax.dynamic_slice_in_dim(query3, first, 2, 1)
        grad_pair = lax.dynamic_slice_in_dim(grad3, first, 2, 1)
        log_pair = lax.dynamic_slice_in_dim(log_all, first, 2, 0)
        delta_pair = lax.dynamic_slice_in_dim(deltas, first, 2, 0)
        scores = pair_scores(query_pair, key_window, visible)
        probabilities = jnp.where(visible[None], jnp.exp(scores - log_pair[:, :, None]), 0.0)
        weights = probabilities.astype(jnp.bfloat16)
        prob_grad = jnp.einsum(
            "tgd,wd->gtw", grad_pair, value_window, preferred_element_type=jnp.float32
        )
        score_grad = (
            probabilities * (prob_grad - delta_pair[:, :, None]) * HEAD_SIZE ** (-0.5)
        ).astype(jnp.bfloat16)
        query_part = jnp.einsum(
            "gtw,wd->tgd", score_grad, key_window, preferred_element_type=jnp.float32
        )
        key_part = jnp.einsum(
            "gtw,tgd->wd", score_grad, query_pair, preferred_element_type=jnp.float32
        )
        value_part = jnp.einsum(
            "gtw,tgd->wd", weights, grad_pair, preferred_element_type=jnp.float32
        )
        query_acc = lax.dynamic_update_slice_in_dim(query_acc, query_part, first, 1)
        old_keys = key_acc
        old_values = value_acc
        key_acc = old_keys + key_part[:, None, :]
        value_acc = old_values + value_part[:, None, :]
        return ((query_acc, key_acc, value_acc), None)

    empty_keys = jnp.zeros((visible_span, kv_heads, HEAD_SIZE), jnp.float32)
    offset_position = (
        jnp.zeros((row_total, head_count, HEAD_SIZE), jnp.float32),
        empty_keys,
        empty_keys,
    )
    (query_acc, key_acc, value_acc), unused = lax.scan(
        backward_step_pair, offset_position, jnp.arange(head_count // 2, dtype=jnp.int32)
    )
    return (query_acc, key_acc, value_acc)


def on_device(queries, keys, values, doc_ids, output_gradient):
    keys_here, values_here = (
        lax.all_to_all(keys, "head", split_axis=1, concat_axis=0, tiled=True),
        lax.all_to_all(values, "head", split_axis=1, concat_axis=0, tiled=True),
    )
    row_total = keys_here.shape[0]
    kv_heads = keys_here.shape[1] // HEAD_SIZE
    head_count = queries.shape[1] // HEAD_SIZE
    margin_rows = SPAN * row_total
    shard_start = lax.axis_index("ctx") * row_total
    key_parts = []
    value_parts = []
    for reach_back in range(SPAN, 0, -1):
        earlier_keys, earlier_values = shifted((keys_here, values_here), "ctx", reach_back)
        key_parts.append(earlier_keys)
        value_parts.append(earlier_values)
    key_window = jnp.concatenate(key_parts + [keys_here], 0)
    value_window = jnp.concatenate(value_parts + [values_here], 0)
    visible = doc_visible(
        doc_ids,
        shard_start,
        shard_start - margin_rows,
        row_total,
        margin_rows + row_total,
        margin_rows,
    )
    query3 = queries.reshape(row_total, head_count, HEAD_SIZE)
    grad3 = output_gradient.reshape(row_total, head_count, HEAD_SIZE)
    attended3, log_all = forward_heads(query3, key_window, value_window, visible)
    deltas = jnp.einsum("thd,thd->ht", grad3, attended3, preferred_element_type=jnp.float32)
    query_acc, key_acc, value_acc = backward_heads(
        query3, grad3, log_all, deltas, key_window, value_window, visible
    )
    own_keys = key_acc[margin_rows:]
    own_values = value_acc[margin_rows:]
    for reach_back in range(1, SPAN + 1):
        lower = margin_rows - reach_back * row_total
        got_keys, got_values = (
            shifted(
                key_acc[lower : lower + row_total].astype(jnp.bfloat16), "ctx", -reach_back
            ).astype(jnp.float32),
            shifted(
                value_acc[lower : lower + row_total].astype(jnp.bfloat16), "ctx", -reach_back
            ).astype(jnp.float32),
        )
        own_keys = own_keys + got_keys
        own_values = own_values + got_values
    key_rounded = own_keys.reshape(row_total, kv_heads * HEAD_SIZE).astype(jnp.bfloat16)
    value_rounded = own_values.reshape(row_total, kv_heads * HEAD_SIZE).astype(jnp.bfloat16)
    key_result, value_result = (
        lax.all_to_all(key_rounded, "head", split_axis=0, concat_axis=1, tiled=True),
        lax.all_to_all(value_rounded, "head", split_axis=0, concat_axis=1, tiled=True),
    )
    attended = attended3.reshape(row_total, head_count * HEAD_SIZE)
    query_grad = query_acc.reshape(row_total, head_count * HEAD_SIZE).astype(jnp.bfloat16)
    return (attended, query_grad, key_result, value_result)


def solution(mesh):
    in_specs = (
        P("ctx", "head"),
        P(("ctx", "head"), None),
        P(("ctx", "head"), None),
        P(),
        P("ctx", "head"),
    )
    out_specs = (
        P("ctx", "head"),
        P("ctx", "head"),
        P(("ctx", "head"), None),
        P(("ctx", "head"), None),
    )
    return jax.shard_map(
        on_device, mesh=mesh, in_specs=in_specs, out_specs=out_specs, check_vma=False
    )
```

profile of v0, /device:TPU:33, one launch (start us, length us, event | category | flops | bytes accessed | tf_op | source)
XLA Modules:
  0.0 211.5 jit_solution(5791085534462519577)
XLA Ops:
  2.1 28.1 %all-to-all-start.1 = ((bf16[32,8,128]{2,0,1:T(8,128)(2,1)}), bf16[32,8,128]{2,0,1:T(8,128)(2,1)S(1)}, u32[]{:S(2)}, u32[]{:S(2)}) async-start(bf16[32,8,128]{2,0,1:T(8,128)(2,1)} %copy_bitcast_fusion.4), calls=%async_computation.1 | async-start | bytes 131072 | tf_op jit(solution)/shard_map/all_to_all | solution.py:122
  30.2 1.5 copy_bitcast_fusion.5
  31.7 23.5 %all-to-all-done.1 = bf16[32,8,128]{2,0,1:T(8,128)(2,1)S(1)} async-done(((bf16[32,8,128]{2,0,1:T(8,128)(2,1)}), bf16[32,8,128]{2,0,1:T(8,128)(2,1)S(1)}, u32[]{:S(2)}, u32[]{:S(2)}) %all-to-all-start.1) | async-done | bytes 65568 | tf_op jit(solution)/shard_map/all_to_all | solution.py:122
  55.2 4.0 %all-to-all-start = ((bf16[32,8,128]{2,0,1:T(8,128)(2,1)}), bf16[32,8,128]{2,0,1:T(8,128)(2,1)S(1)}, u32[]{:S(2)}, u32[]{:S(2)}) async-start(bf16[32,8,128]{2,0,1:T(8,128)(2,1)} %copy_bitcast_fusion.5), calls=%async_computation | async-start | bytes 131072 | tf_op jit(solution)/shard_map/all_to_all | solution.py:121
  62.1 3.1 %collective-permute-start.3 = (bf16[256,128]{1,0:T(8,128)(2,1)S(1)}, bf16[256,128]{1,0:T(8,128)(2,1)S(1)}, u32[]{:S(2)}, u32[]{:S(2)}) collective-permute-start(bf16[256,128]{1,0:T(8,128)(2,1)S(1)} %bitcast.155), channel_id=1, source_target_pairs={{0,8},{8,16},{16,24},{24,32},{32,40},{40,48},{48,56},{56,64},{64,7... | collective-permute-start | bytes 196616 | tf_op jit(solution)/shard_map/ppermute | solution.py:16
  65.2 4.4 %collective-permute-start.2 = (bf16[256,128]{1,0:T(8,128)(2,1)S(1)}, bf16[256,128]{1,0:T(8,128)(2,1)S(1)}, u32[]{:S(2)}, u32[]{:S(2)}) collective-permute-start(bf16[256,128]{1,0:T(8,128)(2,1)S(1)} %bitcast.156), channel_id=1, source_target_pairs={{0,16},{8,24},{16,32},{24,40},{32,48},{40,56},{48,64},{56,72},{64,... | collective-permute-start | bytes 196616 | tf_op jit(solution)/shard_map/ppermute | solution.py:16
  69.6 13.9 %all-to-all-done = bf16[32,8,128]{2,0,1:T(8,128)(2,1)S(1)} async-done(((bf16[32,8,128]{2,0,1:T(8,128)(2,1)}), bf16[32,8,128]{2,0,1:T(8,128)(2,1)S(1)}, u32[]{:S(2)}, u32[]{:S(2)}) %all-to-all-start) | async-done | bytes 65568 | tf_op jit(solution)/shard_map/all_to_all | solution.py:121
  83.5 3.1 %collective-permute-start.1 = (bf16[256,128]{1,0:T(8,128)(2,1)S(1)}, bf16[256,128]{1,0:T(8,128)(2,1)S(1)}, u32[]{:S(2)}, u32[]{:S(2)}) collective-permute-start(bf16[256,128]{1,0:T(8,128)(2,1)S(1)} %bitcast.158), channel_id=1, source_target_pairs={{0,8},{8,16},{16,24},{24,32},{32,40},{40,48},{48,56},{56,64},{64,7... | collective-permute-start | bytes 196616 | tf_op jit(solution)/shard_map/ppermute | solution.py:16
  86.6 4.4 %collective-permute-start = (bf16[256,128]{1,0:T(8,128)(2,1)S(1)}, bf16[256,128]{1,0:T(8,128)(2,1)S(1)}, u32[]{:S(2)}, u32[]{:S(2)}) collective-permute-start(bf16[256,128]{1,0:T(8,128)(2,1)S(1)} %bitcast.159), channel_id=1, source_target_pairs={{0,16},{8,24},{16,32},{24,40},{32,48},{40,56},{48,64},{56,72},{64,... | collective-permute-start | bytes 196616 | tf_op jit(solution)/shard_map/ppermute | solution.py:16
  91.1 1.7 collective-permute-done.1
  92.7 3.4 %collective-permute-done = bf16[256,128]{1,0:T(8,128)(2,1)S(1)} collective-permute-done((bf16[256,128]{1,0:T(8,128)(2,1)S(1)}, bf16[256,128]{1,0:T(8,128)(2,1)S(1)}, u32[]{:S(2)}, u32[]{:S(2)}) %collective-permute-start) | collective-permute-done | bytes 65568 | tf_op jit(solution)/shard_map/ppermute | solution.py:16
  96.3 12.1 %while.28 = (s32[]{:T(128)}, bf16[256,8,128]{2,0,1:T(8,128)(2,1)S(1)}, f32[8,256]{1,0:T(8,128)S(1)}, s32[4]{0:T(128)S(1)}, bf16[256,8,128]{2,0,1:T(8,128)(2,1)S(...) while((s32[]{:T(128)}, ...), condition=%wide.region_3.4_spmd.clone, body=%wide.region_0.3_spmd.clone.sunk | while | flops 205127168 | bytes 5988571 | solution.py:63
  109.4 2.6 %copy.61 = f32[8,256,128]{1,2,0:T(8,128)} copy(f32[8,256,128]{2,1,0:T(8,128)} %bitcast_convert_fusion) | data formatting | bytes 2097152
  113.4 16.1 %while.29 = (s32[]{:T(128)}, bf16[256,8,128]{2,0,1:T(8,128)(2,1)S(1)}, f32[768,1,128]{2,0,1:T(8,128)S(1)}, f32[768,1,128]{2,0,1:T(8,128)S(1)}, s32[4]{0:T(128)S(...) while((s32[]{:T(128)}, ...), condition=%wide.region_5.6_spmd.clone, body=%wide.region_4.5_spmd.clone.sunk | while | flops 507838464 | bytes 10637586 | solution.py:113
  129.6 3.4 %collective-permute-start.6 = (bf16[256,1,128]{2,0,1:T(8,128)(2,1)S(1)}, bf16[256,1,128]{2,0,1:T(8,128)(2,1)S(1)}, u32[]{:S(2)}, u32[]{:S(2)}) collective-permute-start(bf16[256,1,128]{2,0,1:T(8,128)(2,1)S(1)} %get-tuple-element.334), channel_id=1, source_target_pairs={{8,0},{16,8},{24,16},{32,24},{40,32},{48,40},{56,48},{64,56},{72,6... | collective-permute-start | bytes 196616 | tf_op jit(solution)/shard_map/ppermute | solution.py:16
  133.0 1.9 collective-permute-start.7
  135.0 4.5 %collective-permute-done.7 = bf16[256,1,128]{2,0,1:T(8,128)(2,1)S(1)} collective-permute-done((bf16[256,1,128]{2,0,1:T(8,128)(2,1)S(1)}, bf16[256,1,128]{2,0,1:T(8,128)(2,1)S(1)}, u32[]{:S(2)}, u32[]{:S(2)}) %collective-permute-start.7) | collective-permute-done | bytes 65568 | tf_op jit(solution)/shard_map/ppermute | solution.py:16
  140.2 11.1 %all-to-all-start.3 = ((bf16[8,32,128]{2,1,0:T(8,128)(2,1)}), bf16[8,32,128]{2,1,0:T(8,128)(2,1)S(1)}, u32[]{:S(2)}, u32[]{:S(2)}) async-start(bf16[8,32,128]{2,1,0:T(8,128)(2,1)} %bitcast.14), calls=%async_computation.3 | async-start | bytes 131072 | tf_op jit(solution)/shard_map/all_to_all | solution.py:170
  151.3 4.9 %collective-permute-start.4 = (bf16[256,1,128]{2,0,1:T(8,128)(2,1)S(1)}, bf16[256,1,128]{2,0,1:T(8,128)(2,1)S(1)}, u32[]{:S(2)}, u32[]{:S(2)}) collective-permute-start(bf16[256,1,128]{2,0,1:T(8,128)(2,1)S(1)} %get-tuple-element.336), channel_id=1, source_target_pairs={{8,0},{16,8},{24,16},{32,24},{40,32},{48,40},{56,48},{64,56},{72,6... | collective-permute-start | bytes 196616 | tf_op jit(solution)/shard_map/ppermute | solution.py:16
  156.2 2.2 %collective-permute-start.5 = (bf16[256,1,128]{2,0,1:T(8,128)(2,1)S(1)}, bf16[256,1,128]{2,0,1:T(8,128)(2,1)S(1)}, u32[]{:S(2)}, u32[]{:S(2)}) collective-permute-start(bf16[256,1,128]{2,0,1:T(8,128)(2,1)S(1)} %get-tuple-element.337), channel_id=1, source_target_pairs={{16,0},{24,8},{32,16},{40,24},{48,32},{56,40},{64,48},{72,56},{80,... | collective-permute-start | bytes 196616 | tf_op jit(solution)/shard_map/ppermute | solution.py:16
  158.4 4.6 %collective-permute-done.5 = bf16[256,1,128]{2,0,1:T(8,128)(2,1)S(1)} collective-permute-done((bf16[256,1,128]{2,0,1:T(8,128)(2,1)S(1)}, bf16[256,1,128]{2,0,1:T(8,128)(2,1)S(1)}, u32[]{:S(2)}, u32[]{:S(2)}) %collective-permute-start.5) | collective-permute-done | bytes 65568 | tf_op jit(solution)/shard_map/ppermute | solution.py:16
  163.6 11.8 %all-to-all-done.3 = bf16[8,32,128]{2,1,0:T(8,128)(2,1)S(1)} async-done(((bf16[8,32,128]{2,1,0:T(8,128)(2,1)}), bf16[8,32,128]{2,1,0:T(8,128)(2,1)S(1)}, u32[]{:S(2)}, u32[]{:S(2)}) %all-to-all-start.3) | async-done | bytes 65568 | tf_op jit(solution)/shard_map/all_to_all | solution.py:170
  175.5 11.0 %all-to-all-start.2 = ((bf16[8,32,128]{2,1,0:T(8,128)(2,1)}), bf16[8,32,128]{2,1,0:T(8,128)(2,1)S(1)}, u32[]{:S(2)}, u32[]{:S(2)}) async-start(bf16[8,32,128]{2,1,0:T(8,128)(2,1)} %bitcast.12), calls=%async_computation.2 | async-start | bytes 131072 | tf_op jit(solution)/shard_map/all_to_all | solution.py:169
  188.2 22.7 %all-to-all-done.2 = bf16[8,32,128]{2,1,0:T(8,128)(2,1)S(1)} async-done(((bf16[8,32,128]{2,1,0:T(8,128)(2,1)}), bf16[8,32,128]{2,1,0:T(8,128)(2,1)S(1)}, u32[]{:S(2)}, u32[]{:S(2)}) %all-to-all-start.2) | async-done | bytes 65568 | tf_op jit(solution)/shard_map/all_to_all | solution.py:169
  (95 shorter events, 33.2 us)
Async XLA Ops:
  0.6 0.8 copy-start
  1.5 60.1 %copy-start.1 = (bf16[256,1024]{1,0:T(8,128)(2,1)S(1)}, bf16[256,1024]{1,0:T(8,128)(2,1)}, u32[]{:S(2)}) copy-start(bf16[256,1024]{1,0:T(8,128)(2,1)} %param.9) | copy-start | bytes 1572868
  2.1 53.1 %all-to-all-start.1 = ((bf16[32,8,128]{2,0,1:T(8,128)(2,1)}), bf16[32,8,128]{2,0,1:T(8,128)(2,1)S(1)}, u32[]{:S(2)}, u32[]{:S(2)}) async-start(bf16[32,8,128]{2,0,1:T(8,128)(2,1)} %copy_bitcast_fusion.4), calls=%async_computation.1 | async-start | bytes 131072 | tf_op jit(solution)/shard_map/all_to_all | solution.py:122
  55.2 28.4 %all-to-all-start = ((bf16[32,8,128]{2,0,1:T(8,128)(2,1)}), bf16[32,8,128]{2,0,1:T(8,128)(2,1)S(1)}, u32[]{:S(2)}, u32[]{:S(2)}) async-start(bf16[32,8,128]{2,0,1:T(8,128)(2,1)} %copy_bitcast_fusion.5), calls=%async_computation | async-start | bytes 131072 | tf_op jit(solution)/shard_map/all_to_all | solution.py:121
  62.1 28.9 %collective-permute-start.3 = (bf16[256,128]{1,0:T(8,128)(2,1)S(1)}, bf16[256,128]{1,0:T(8,128)(2,1)S(1)}, u32[]{:S(2)}, u32[]{:S(2)}) collective-permute-start(bf16[256,128]{1,0:T(8,128)(2,1)S(1)} %bitcast.155), channel_id=1, source_target_pairs={{0,8},{8,16},{16,24},{24,32},{32,40},{40,48},{48,56},{56,64},{64,7... | collective-permute-start | bytes 196616 | tf_op jit(solution)/shard_map/ppermute | solution.py:16
  65.2 25.8 %collective-permute-start.2 = (bf16[256,128]{1,0:T(8,128)(2,1)S(1)}, bf16[256,128]{1,0:T(8,128)(2,1)S(1)}, u32[]{:S(2)}, u32[]{:S(2)}) collective-permute-start(bf16[256,128]{1,0:T(8,128)(2,1)S(1)} %bitcast.156), channel_id=1, source_target_pairs={{0,16},{8,24},{16,32},{24,40},{32,48},{40,56},{48,64},{56,72},{64,... | collective-permute-start | bytes 196616 | tf_op jit(solution)/shard_map/ppermute | solution.py:16
  83.5 9.2 %collective-permute-start.1 = (bf16[256,128]{1,0:T(8,128)(2,1)S(1)}, bf16[256,128]{1,0:T(8,128)(2,1)S(1)}, u32[]{:S(2)}, u32[]{:S(2)}) collective-permute-start(bf16[256,128]{1,0:T(8,128)(2,1)S(1)} %bitcast.158), channel_id=1, source_target_pairs={{0,8},{8,16},{16,24},{24,32},{32,40},{40,48},{48,56},{56,64},{64,7... | collective-permute-start | bytes 196616 | tf_op jit(solution)/shard_map/ppermute | solution.py:16
  86.6 9.5 %collective-permute-start = (bf16[256,128]{1,0:T(8,128)(2,1)S(1)}, bf16[256,128]{1,0:T(8,128)(2,1)S(1)}, u32[]{:S(2)}, u32[]{:S(2)}) collective-permute-start(bf16[256,128]{1,0:T(8,128)(2,1)S(1)} %bitcast.159), channel_id=1, source_target_pairs={{0,16},{8,24},{16,32},{24,40},{32,48},{40,56},{48,64},{56,72},{64,... | collective-permute-start | bytes 196616 | tf_op jit(solution)/shard_map/ppermute | solution.py:16
  129.6 5.3 %collective-permute-start.6 = (bf16[256,1,128]{2,0,1:T(8,128)(2,1)S(1)}, bf16[256,1,128]{2,0,1:T(8,128)(2,1)S(1)}, u32[]{:S(2)}, u32[]{:S(2)}) collective-permute-start(bf16[256,1,128]{2,0,1:T(8,128)(2,1)S(1)} %get-tuple-element.334), channel_id=1, source_target_pairs={{8,0},{16,8},{24,16},{32,24},{40,32},{48,40},{56,48},{64,56},{72,6... | collective-permute-start | bytes 196616 | tf_op jit(solution)/shard_map/ppermute | solution.py:16
  133.0 6.5 %collective-permute-start.7 = (bf16[256,1,128]{2,0,1:T(8,128)(2,1)S(1)}, bf16[256,1,128]{2,0,1:T(8,128)(2,1)S(1)}, u32[]{:S(2)}, u32[]{:S(2)}) collective-permute-start(bf16[256,1,128]{2,0,1:T(8,128)(2,1)S(1)} %get-tuple-element.335), channel_id=1, source_target_pairs={{16,0},{24,8},{32,16},{40,24},{48,32},{56,40},{64,48},{72,56},{80,... | collective-permute-start | bytes 196616 | tf_op jit(solution)/shard_map/ppermute | solution.py:16
  140.2 35.3 %all-to-all-start.3 = ((bf16[8,32,128]{2,1,0:T(8,128)(2,1)}), bf16[8,32,128]{2,1,0:T(8,128)(2,1)S(1)}, u32[]{:S(2)}, u32[]{:S(2)}) async-start(bf16[8,32,128]{2,1,0:T(8,128)(2,1)} %bitcast.14), calls=%async_computation.3 | async-start | bytes 131072 | tf_op jit(solution)/shard_map/all_to_all | solution.py:170
  151.3 7.1 %collective-permute-start.4 = (bf16[256,1,128]{2,0,1:T(8,128)(2,1)S(1)}, bf16[256,1,128]{2,0,1:T(8,128)(2,1)S(1)}, u32[]{:S(2)}, u32[]{:S(2)}) collective-permute-start(bf16[256,1,128]{2,0,1:T(8,128)(2,1)S(1)} %get-tuple-element.336), channel_id=1, source_target_pairs={{8,0},{16,8},{24,16},{32,24},{40,32},{48,40},{56,48},{64,56},{72,6... | collective-permute-start | bytes 196616 | tf_op jit(solution)/shard_map/ppermute | solution.py:16
  156.2 6.8 %collective-permute-start.5 = (bf16[256,1,128]{2,0,1:T(8,128)(2,1)S(1)}, bf16[256,1,128]{2,0,1:T(8,128)(2,1)S(1)}, u32[]{:S(2)}, u32[]{:S(2)}) collective-permute-start(bf16[256,1,128]{2,0,1:T(8,128)(2,1)S(1)} %get-tuple-element.337), channel_id=1, source_target_pairs={{16,0},{24,8},{32,16},{40,24},{48,32},{56,40},{64,48},{72,56},{80,... | collective-permute-start | bytes 196616 | tf_op jit(solution)/shard_map/ppermute | solution.py:16
  175.5 35.4 %all-to-all-start.2 = ((bf16[8,32,128]{2,1,0:T(8,128)(2,1)}), bf16[8,32,128]{2,1,0:T(8,128)(2,1)S(1)}, u32[]{:S(2)}, u32[]{:S(2)}) async-start(bf16[8,32,128]{2,1,0:T(8,128)(2,1)} %bitcast.12), calls=%async_computation.2 | async-start | bytes 131072 | tf_op jit(solution)/shard_map/all_to_all | solution.py:169
where the time goes:
time: 213 us; the launch traced here: 212 us
  waiting for transfers between devices  86.2 us (40%)
  starting transfers between devices  81.5 us (38%)
  local copies, waits for them, and re-layouts  14.7 us (7%)
  matrix products  14.3 us (7%)
  other arithmetic  8.25 us (4%)
  loops' own time  5.63 us (3%)
    all_to_all x1, starting transfers between devices, on_device(): lax.all_to_all(values, 'head', split_axis=1, concat_axis=0, tiled=True)  28.1 us
    ppermute x8, starting transfers between devices, shifted(): return lax.ppermute(x, axis, pairs)  27.3 us
    all_to_all x1, waiting for transfers between devices, on_device(): lax.all_to_all(values, 'head', split_axis=1, concat_axis=0, tiled=True)  23.5 us
    all_to_all x1, waiting for transfers between devices, on_device(): lax.all_to_all(key_rounded, 'head', split_axis=0, concat_axis=1, tiled=True)  22.7 us
    ppermute x8, waiting for transfers between devices, shifted(): return lax.ppermute(x, axis, pairs)  14.3 us
    all_to_all x1, waiting for transfers between devices, on_device(): lax.all_to_all(keys, 'head', split_axis=1, concat_axis=0, tiled=True)  13.9 us
    all_to_all x1, waiting for transfers between devices, on_device(): lax.all_to_all(value_rounded, 'head', split_axis=0, concat_axis=1, tiled=...  11.8 us
    all_to_all x1, starting transfers between devices, on_device(): lax.all_to_all(value_rounded, 'head', split_axis=0, concat_axis=1, tiled=...  11.1 us
  transfers between devices with their start and end apart: 12, of which 8 were waited for; matrix products, arithmetic and copies ran while one was open for 3% of the time, Pallas kernels for 0%

commit v1 on v0

v1 whole, which is shorter than its diff:
```python
import functools
import math

import jax
import jax.numpy as jnp
from jax import lax
from jax.experimental import pallas as pl
from jax.experimental.pallas import tpu as pltpu
from jax.sharding import PartitionSpec as P

HEAD_SIZE = 128
TILE = 128
SPAN = 2
GROUPS = 4
SCALE = HEAD_SIZE ** -0.5
EXP2_SCALE = SCALE * math.log2(math.e)
MASKED = -1e30
MESH = pl.DeviceIdType.MESH
F32 = jnp.float32
BF16 = jnp.bfloat16


def dot_nt(a, b):
    return lax.dot_general(a, b, (((1,), (1,)), ((), ())), preferred_element_type=F32)


def dot_nn(a, b):
    return lax.dot_general(a, b, (((1,), (0,)), ((), ())), preferred_element_type=F32)


def kernel(
    n_ctx,
    q_hbm,
    k_hbm,
    v_hbm,
    doc_hbm,
    g_hbm,
    att_hbm,
    dq_hbm,
    dk_hbm,
    dv_hbm,
    stage,
    window,
    relay,
    doc,
    qs,
    gs,
    qt,
    gt,
    bias,
    probs,
    weights,
    score_grad,
    att_out,
    dq_out,
    acc,
    part,
    own,
    got,
    home,
    back_relay,
    result,
    load_sem,
    head_load_sem,
    self_sem,
    out_sem,
    result_sem,
    fwd_send,
    fwd_recv,
    fwd_relay_recv,
    ctx_send,
    ctx_recv,
    back_ctx_send,
    back_ctx_recv,
    back_send,
    back_recv,
    back_relay_recv,
):
    rows = TILE * 2
    piece = stage.shape[1]
    group_rows = 2 * piece
    heads = qs.shape[1] // TILE
    reach = SPAN * rows + TILE
    ctx = lax.axis_index("ctx")
    head = lax.axis_index("head")
    zone = head // 2
    core = lax.rem(head, 2)

    def zone_at(offset):
        return lax.rem(zone + offset, GROUPS)

    far, plus, minus = zone_at(2), zone_at(1), zone_at(3)
    relative = (far, plus, minus, zone)
    partner = zone * 2 + (1 - core)

    has_later = (ctx + 1 < n_ctx, ctx + 2 < n_ctx)
    has_earlier = (ctx >= 1, ctx >= 2)

    barrier = pltpu.get_barrier_semaphore()
    for peer in (plus * 2, plus * 2 + 1, minus * 2, minus * 2 + 1, partner):
        pl.semaphore_signal(barrier, inc=1, device_id=(ctx, peer), device_id_type=MESH)
    for dist in (1, 2):

        @pl.when(has_later[dist - 1])
        def _():
            pl.semaphore_signal(
                barrier, inc=1, device_id=(ctx + dist, head), device_id_type=MESH
            )

        @pl.when(has_earlier[dist - 1])
        def _():
            pl.semaphore_signal(
                barrier, inc=1, device_id=(ctx - dist, head), device_id_type=MESH
            )

    loads = [
        pltpu.make_async_copy(k_hbm, stage.at[0], load_sem.at[0]),
        pltpu.make_async_copy(v_hbm, stage.at[1], load_sem.at[1]),
        pltpu.make_async_copy(doc_hbm, doc, load_sem.at[2]),
    ]
    for copy in loads:
        copy.start()
    head_loads = []
    for which, (source, target) in enumerate(((q_hbm, qs), (g_hbm, gs))):
        for i in range(2):
            for h in range(heads):
                copy = pltpu.make_async_copy(
                    source.at[pl.ds(i * TILE, TILE), pl.ds(h * TILE, TILE)],
                    target.at[i, pl.ds(h * TILE, TILE), :],
                    head_load_sem.at[which, i, h],
                )
                copy.start()
                head_loads.append(copy)

    zero_block = jnp.zeros((rows, HEAD_SIZE), BF16)

    @pl.when(ctx < 1)
    def _():
        for a in range(2):
            window[a, pl.ds(rows, rows), :] = zero_block

    @pl.when(ctx < 2)
    def _():
        for a in range(2):
            window[a, pl.ds(0, rows), :] = zero_block

    for dist in (1, 2):

        @pl.when(ctx + dist >= n_ctx)
        def _():
            for a in range(2):
                got[a, dist - 1] = zero_block

    acc[...] = jnp.zeros_like(acc)

    def columns(of_head):
        return pl.ds(pl.multiple_of(of_head * HEAD_SIZE, HEAD_SIZE), HEAD_SIZE)

    def piece_rows(of_head, base=0):
        return pl.ds(pl.multiple_of(base + of_head * piece, piece), piece)

    def zone_rows(of_zone, base=0):
        return pl.ds(pl.multiple_of(base + of_zone * group_rows, group_rows), group_rows)

    loads[0].wait()
    loads[1].wait()
    self_copies = []
    for a in range(2):
        copy = pltpu.make_async_copy(
            stage.at[a, :, columns(head)],
            window.at[a, piece_rows(head, SPAN * rows), :],
            self_sem.at[a],
        )
        copy.start()
        self_copies.append(copy)
    loads[2].wait()

    row_place = lax.broadcasted_iota(jnp.int32, (TILE, TILE), 0)
    column_place = lax.broadcasted_iota(jnp.int32, (TILE, TILE), 1)
    for i in range(2):
        query_docs = jnp.broadcast_to(
            doc[pl.ds(2 * ctx + i, 1), :].astype(F32), (TILE, TILE)
        ).T
        for j in range(5):
            doc_row = 2 * ctx - 2 * SPAN + i + j
            key_docs = doc[pl.ds(jnp.maximum(doc_row, 0), 1), :].astype(F32)
            seen = query_docs == key_docs
            if j == 4:
                seen = seen & (column_place <= row_place)
            outside = jnp.where(doc_row >= 0, 0.0, MASKED).astype(F32)
            bias[i, :, pl.ds(j * TILE, TILE)] = jnp.where(seen, 0.0, MASKED) + outside

    for copy in head_loads:
        copy.wait()
    for i in range(2):
        for h in range(heads):
            at = pl.ds(h * TILE, TILE)
            qt[i, :, at] = qs[i, at, :].T
            gt[i, :, at] = gs[i, at, :].T

    pl.semaphore_wait(
        barrier,
        5
        + has_later[0].astype(jnp.int32)
        + has_later[1].astype(jnp.int32)
        + has_earlier[0].astype(jnp.int32)
        + has_earlier[1].astype(jnp.int32),
    )

    sends = []

    def remote(source, target, send_sem, recv_sem, device):
        return pltpu.make_async_remote_copy(
            src_ref=source,
            dst_ref=target,
            send_sem=send_sem,
            recv_sem=recv_sem,
            device_id=device,
            device_id_type=MESH,
        )

    def send(source, target, send_sem, recv_sem, device):
        copy = remote(source, target, send_sem, recv_sem, device)
        copy.start()
        sends.append((copy, None))

    def send_if(wanted, source, target, send_sem, recv_sem, device):
        copy = remote(source, target, send_sem, recv_sem, device)

        @pl.when(wanted)
        def _():
            copy.start()

        sends.append((copy, wanted))

    def arrived(target, recv_sem):
        remote(target, target, fwd_send.at[0, 0], recv_sem, (ctx, partner)).wait_recv()

    def exchange_far(source_of, relay_ref, send_sem, recv_sem):
        for way, (middle, target_core) in enumerate(((plus, core), (minus, 1 - core))):
            send(
                source_of(far * 2 + target_core),
                relay_ref.at[way],
                send_sem.at[way],
                recv_sem.at[way],
                (ctx, middle * 2 + target_core),
            )

    def exchange_near(source_of, target, zone_number, send_sem, recv_sem, slot):
        for target_core in range(2):
            peer = zone_number * 2 + target_core
            send(source_of(peer), target, send_sem.at[slot + target_core], recv_sem, (ctx, peer))

    def pass_on(relay_ref, target_of, send_sem, relay_recv, recv_of):
        for way, (after, origin) in enumerate(
            ((plus, minus * 2 + core), (minus, plus * 2 + (1 - core)))
        ):
            arrived(relay_ref.at[way], relay_recv.at[way])
            send(
                relay_ref.at[way],
                target_of(origin),
                send_sem.at[7 + way],
                recv_of(origin),
                (ctx, after * 2 + core),
            )

    for a in range(2):
        source_of = lambda to_head: stage.at[a, :, columns(to_head)]
        mine = window.at[a, piece_rows(head, SPAN * rows), :]
        exchange_far(source_of, relay.at[a], fwd_send.at[a], fwd_relay_recv.at[a])
        exchange_near(source_of, mine, plus, fwd_send.at[a], fwd_recv.at[a, head], 2)
        exchange_near(source_of, mine, minus, fwd_send.at[a], fwd_recv.at[a, head], 4)
        send(
            source_of(partner), mine, fwd_send.at[a, 6], fwd_recv.at[a, head], (ctx, partner)
        )

    def window_piece(a, of_head):
        return window.at[a, piece_rows(of_head, SPAN * rows), :]

    def hand_on(a, r):
        group = relative[r]
        if r == 3:
            self_copies[a].wait()
            arrived(window_piece(a, partner), fwd_recv.at[a, partner])
        else:
            for source_core in range(2):
                origin = group * 2 + source_core
                arrived(window_piece(a, origin), fwd_recv.at[a, origin])
        for dist in (1, 2):
            send_if(
                has_later[dist - 1],
                window.at[a, zone_rows(group, SPAN * rows), :],
                window.at[a, zone_rows(group, (SPAN - dist) * rows), :],
                ctx_send.at[a, dist - 1, r],
                ctx_recv.at[a, dist - 1, r],
                (ctx + dist, head),
            )

    def relay_forward(a):
        pass_on(
            relay.at[a],
            lambda origin: window_piece(a, origin),
            fwd_send.at[a],
            fwd_relay_recv.at[a],
            lambda origin: fwd_recv.at[a, origin],
        )

    hand_on(0, 3)
    hand_on(1, 3)
    relay_forward(0)
    hand_on(0, 1)
    hand_on(0, 2)
    relay_forward(1)
    hand_on(1, 1)
    hand_on(1, 2)
    hand_on(0, 0)
    hand_on(1, 0)

    def window_here(a):
        for r in (3, 1, 2, 0):
            for dist in (1, 2):

                @pl.when(has_earlier[dist - 1])
                def _():
                    arrived(
                        window.at[a, zone_rows(relative[r], (SPAN - dist) * rows), :],
                        ctx_recv.at[a, dist - 1, r],
                    )

    blocks = heads // 2

    def block_of(n):
        i = n // blocks
        at = pl.ds(pl.multiple_of(lax.rem(n, blocks) * (2 * TILE), 2 * TILE), 2 * TILE)
        span = pl.ds(pl.multiple_of(i * TILE, TILE), reach)
        return i, at, span

    window_here(0)

    def probability_step(n, carry):
        i, at, span = block_of(n)
        scores = dot_nt(qs[i, at, :], window[0, span, :])
        mask = bias[i]
        scores = scores + jnp.concatenate([mask, mask], 0)
        row_max = jnp.max(scores, axis=1, keepdims=True)
        raised = jnp.exp2((scores - row_max) * EXP2_SCALE)
        inverse = 1.0 / jnp.sum(raised, axis=1, keepdims=True)
        probability = raised * inverse
        probs[i, at, :] = probability
        weights[i, at, :] = probability.astype(BF16)
        return carry

    lax.fori_loop(0, 2 * blocks, probability_step, 0)

    def collect(g, left, right):
        for i in range(2):
            span = pl.ds(i * TILE, reach)
            acc[g, :, span] = acc[g, :, span] + dot_nn(left[i], right[i])
        for t in range(2 * SPAN + 2):
            block = acc[g, :, pl.ds(t * TILE, TILE)].T
            if t < 2 * SPAN:
                part[g, pl.ds(t * TILE, TILE), :] = block.astype(BF16)
            else:
                own[g, pl.ds(t * TILE - SPAN * rows, TILE), :] = block
        for r in range(GROUPS):
            for dist in (1, 2):
                send_if(
                    has_earlier[dist - 1],
                    part.at[g, zone_rows(relative[r], (SPAN - dist) * rows), :],
                    got.at[g, dist - 1, zone_rows(relative[r]), :],
                    back_ctx_send.at[g, dist - 1, r],
                    back_ctx_recv.at[g, dist - 1, r],
                    (ctx - dist, head),
                )

    collect(1, gt, weights)

    window_here(1)

    def gradient_step(n, carry):
        i, at, span = block_of(n)
        value_window = window[1, span, :]
        out_gradient = gs[i, at, :]
        attended = dot_nn(weights[i, at, :], value_window).astype(BF16)
        att_out[i, at, :] = attended
        delta = jnp.sum(
            out_gradient.astype(F32) * attended.astype(F32), axis=1, keepdims=True
        )
        prob_grad = dot_nt(out_gradient, value_window)
        score_grad[i, at, :] = (probs[i, at, :] * (prob_grad - delta) * SCALE).astype(BF16)
        return carry

    lax.fori_loop(0, 2 * blocks, gradient_step, 0)
    collect(0, qt, score_grad)

    outs = []

    def write_out(which, source, target):
        for i in range(2):
            for h in range(heads):
                copy = pltpu.make_async_copy(
                    source.at[i, pl.ds(h * TILE, TILE), :],
                    target.at[pl.ds(i * TILE, TILE), pl.ds(h * TILE, TILE)],
                    out_sem.at[which, i, h],
                )
                copy.start()
                outs.append(copy)

    write_out(0, att_out, att_hbm)

    self_results = []

    def send_home(g):
        mine = result.at[g, :, columns(head)]
        source_of = lambda to_head: home.at[g, piece_rows(to_head), :]
        for r in range(GROUPS):
            at = zone_rows(relative[r])
            for dist in (1, 2):

                @pl.when(has_later[dist - 1])
                def _():
                    arrived(got.at[g, dist - 1, at, :], back_ctx_recv.at[g, dist - 1, r])

            total = own[g, at, :] + got[g, 0, at, :].astype(F32) + got[g, 1, at, :].astype(F32)
            home[g, at, :] = total.astype(BF16)
            if r == 0:
                exchange_far(source_of, back_relay.at[g], back_send.at[g], back_relay_recv.at[g])
            elif r < 3:
                exchange_near(
                    source_of, mine, relative[r], back_send.at[g], back_recv.at[g, head], 2 * r
                )
            else:
                send(
                    source_of(partner),
                    mine,
                    back_send.at[g, 6],
                    back_recv.at[g, head],
                    (ctx, partner),
                )
                copy = pltpu.make_async_copy(source_of(head), mine, self_sem.at[2 + g])
                copy.start()
                self_results.append(copy)

    def relay_home(g):
        pass_on(
            back_relay.at[g],
            lambda origin: result.at[g, :, columns(origin)],
            back_send.at[g],
            back_relay_recv.at[g],
            lambda origin: back_recv.at[g, origin],
        )

    send_home(1)

    def query_step(n, carry):
        i, at, span = block_of(n)
        dq_out[i, at, :] = dot_nn(score_grad[i, at, :], window[0, span, :]).astype(BF16)
        return carry

    lax.fori_loop(0, 2 * blocks, query_step, 0)
    write_out(1, dq_out, dq_hbm)
    send_home(0)
    relay_home(1)
    relay_home(0)

    for copy in self_results:
        copy.wait()
    for g, target in ((1, dv_hbm), (0, dk_hbm)):
        for r in (3, 1, 2, 0):
            for source_core in range(2):
                origin = relative[r] * 2 + (1 - core if r == 3 else source_core)
                if r == 3 and source_core:
                    continue
                arrived(result.at[g, :, columns(origin)], back_recv.at[g, origin])
        copy = pltpu.make_async_copy(result.at[g], target, result_sem.at[g])
        copy.start()
        outs.append(copy)
    for copy, wanted in sends:
        if wanted is None:
            copy.wait_send()
        else:

            @pl.when(wanted)
            def _():
                copy.wait_send()

    for copy in outs:
        copy.wait()


def on_device(n_ctx, queries, keys, values, doc_ids, output_gradient):
    rows, width = queries.shape
    piece, key_width = keys.shape
    heads = width // HEAD_SIZE
    all_rows = (SPAN + 1) * rows
    stacked = heads * TILE
    reach = SPAN * rows + TILE
    docs = doc_ids.reshape(-1, TILE)
    vmem = pltpu.VMEM
    dma = pltpu.SemaphoreType.DMA
    any_space = pl.BlockSpec(memory_space=pl.ANY)
    return pl.pallas_call(
        functools.partial(kernel, n_ctx),
        out_shape=(
            jax.ShapeDtypeStruct((rows, width), BF16),
            jax.ShapeDtypeStruct((rows, width), BF16),
            jax.ShapeDtypeStruct((piece, key_width), BF16),
            jax.ShapeDtypeStruct((piece, key_width), BF16),
        ),
        in_specs=[any_space] * 5,
        out_specs=(any_space,) * 4,
        scratch_shapes=[
            vmem((2, piece, key_width), BF16),
            vmem((2, all_rows, HEAD_SIZE), BF16),
            vmem((2, 2, piece, HEAD_SIZE), BF16),
            vmem(docs.shape, jnp.int32),
            vmem((2, stacked, HEAD_SIZE), BF16),
            vmem((2, stacked, HEAD_SIZE), BF16),
            vmem((2, HEAD_SIZE, stacked), BF16),
            vmem((2, HEAD_SIZE, stacked), BF16),
            vmem((2, TILE, reach), F32),
            vmem((2, stacked, reach), F32),
            vmem((2, stacked, reach), BF16),
            vmem((2, stacked, reach), BF16),
            vmem((2, stacked, HEAD_SIZE), BF16),
            vmem((2, stacked, HEAD_SIZE), BF16),
            vmem((2, HEAD_SIZE, all_rows), F32),
            vmem((2, SPAN * rows, HEAD_SIZE), BF16),
            vmem((2, rows, HEAD_SIZE), F32),
            vmem((2, SPAN, rows, HEAD_SIZE), BF16),
            vmem((2, rows, HEAD_SIZE), BF16),
            vmem((2, 2, piece, HEAD_SIZE), BF16),
            vmem((2, piece, key_width), BF16),
            dma((3,)),
            dma((2, 2, heads)),
            dma((4,)),
            dma((2, 2, heads)),
            dma((2,)),
            dma((2, 9)),
            dma((2, 2 * GROUPS)),
            dma((2, 2)),
            dma((2, SPAN, GROUPS)),
            dma((2, SPAN, GROUPS)),
            dma((2, SPAN, GROUPS)),
            dma((2, SPAN, GROUPS)),
            dma((2, 9)),
            dma((2, 2 * GROUPS)),
            dma((2, 2)),
        ],
        compiler_params=pltpu.CompilerParams(collective_id=0, has_side_effects=True),
    )(queries, keys, values, docs, output_gradient)


def solution(mesh):
    in_specs = (
        P("ctx", "head"),
        P(("ctx", "head"), None),
        P(("ctx", "head"), None),
        P(),
        P("ctx", "head"),
    )
    out_specs = (
        P("ctx", "head"),
        P("ctx", "head"),
        P(("ctx", "head"), None),
        P(("ctx", "head"), None),
    )
    return jax.shard_map(
        functools.partial(on_device, mesh.shape["ctx"]),
        mesh=mesh,
        in_specs=in_specs,
        out_specs=out_specs,
        check_vma=False,
    )
```

time: 213 us -> 85.6 us (0.40)
  the two profiles are of different devices: /device:TPU:33 before, /device:TPU:124 now
where the time goes in v1:
time: 85.6 us; the launch traced here: 85.3 us
  Pallas kernels  80.3 us (94%)
  local copies, waits for them, and re-layouts  4.28 us (5%)
    pallas_call x1, Pallas kernels, on_device(): pl.pallas_call(functools.partial(kernel, n_ctx), out_shape=(jax.ShapeDtyp...  80.3 us
    unnamed x10, local copies, waits for them, and re-layouts  4.28 us

profile of v1, /device:TPU:124, one launch (start us, length us, event | category | flops | bytes accessed | tf_op | source)
XLA Modules:
  0.0 85.3 jit_solution(9495221010037587815)
XLA Ops:
  0.6 80.3 %shard_map.84 = (bf16[256,1024]{1,0:T(8,128)(2,1)}, bf16[256,1024]{1,0:T(8,128)(2,1)}, bf16[32,1024]{1,0:T(8,128)(2,1)}, bf16[32,1024]{1,0:T(8,128)(2,1)}) custom-call(bf16[256,1024]{1,0:T(8,128)(2,1)} %q_hbm.1, bf16[32,1024]{1,0:T(8,128)(2,1)} %k_hbm.1, bf16[32,1024]{1,0:T(8,128)(2,1)} %v_hbm.1, s32[256,128]{1,0:T(8,128)} %bitcast.1, bf16[256,1024]{1,0:T(8,128)(2,1)} %g_hbm.1), custom_call_target="tpu_custom_call" | custom-call | tf_op jit(solution)/shard_map/pallas_call | solution.py:502
  81.0 0.0 copy-start
  81.0 1.9 %copy.13 = bf16[256,1024]{1,0:T(8,128)(2,1)} copy(bf16[256,1024]{1,0:T(8,128)(2,1)} %get-tuple-element.8) | data formatting | bytes 1048576
  82.9 0.0 copy-done
  82.9 0.0 copy-start.2
  82.9 0.8 copy.14
  83.7 0.1 copy-done.2
  83.8 0.0 copy-start.1
  83.8 0.6 copy.15
  84.4 0.2 copy-done.1
  84.6 0.6 copy.16
Async XLA Ops:
  81.0 1.9 %copy-start = (bf16[256,1024]{1,0:T(8,128)(2,1)S(1)}, bf16[256,1024]{1,0:T(8,128)(2,1)}, u32[]{:S(2)}) copy-start(bf16[256,1024]{1,0:T(8,128)(2,1)} %get-tuple-element.9) | copy-start | bytes 1572868
  82.9 0.9 %copy-start.2 = (bf16[32,1024]{1,0:T(8,128)(2,1)S(1)}, bf16[32,1024]{1,0:T(8,128)(2,1)}, u32[]{:S(2)}) copy-start(bf16[32,1024]{1,0:T(8,128)(2,1)} %get-tuple-element.10) | copy-start | bytes 196612
  83.8 0.9 %copy-start.1 = (bf16[32,1024]{1,0:T(8,128)(2,1)S(1)}, bf16[32,1024]{1,0:T(8,128)(2,1)}, u32[]{:S(2)}) copy-start(bf16[32,1024]{1,0:T(8,128)(2,1)} %get-tuple-element.11) | copy-start | bytes 196612

commit v2 on v1

--- a/solution.py
+++ b/solution.py
@@ -11,10 +11,12 @@
 HEAD_SIZE = 128
 TILE = 128
 SPAN = 2
+BLOCK_HEADS = 2
 GROUPS = 4
 SCALE = HEAD_SIZE ** -0.5
 EXP2_SCALE = SCALE * math.log2(math.e)
 MASKED = -1e30
+LIMIT = 40 << 20
 MESH = pl.DeviceIdType.MESH
 F32 = jnp.float32
 BF16 = jnp.bfloat16
@@ -35,10 +37,10 @@
     v_hbm,
     doc_hbm,
     g_hbm,
-    att_hbm,
-    dq_hbm,
-    dk_hbm,
-    dv_hbm,
+    att_out,
+    dq_out,
+    dk_out,
+    dv_out,
     stage,
     window,
     relay,
@@ -51,8 +53,8 @@
     probs,
     weights,
     score_grad,
-    att_out,
-    dq_out,
+    held,
+    row_held,
     acc,
     part,
     own,
@@ -63,8 +65,6 @@
     load_sem,
     head_load_sem,
     self_sem,
-    out_sem,
-    result_sem,
     fwd_send,
     fwd_recv,
     fwd_relay_recv,
@@ -120,38 +120,6 @@
     ]
     for copy in loads:
         copy.start()
-    head_loads = []
-    for which, (source, target) in enumerate(((q_hbm, qs), (g_hbm, gs))):
-        for i in range(2):
-            for h in range(heads):
-                copy = pltpu.make_async_copy(
-                    source.at[pl.ds(i * TILE, TILE), pl.ds(h * TILE, TILE)],
-                    target.at[i, pl.ds(h * TILE, TILE), :],
-                    head_load_sem.at[which, i, h],
-                )
-                copy.start()
-                head_loads.append(copy)
-
-    zero_block = jnp.zeros((rows, HEAD_SIZE), BF16)
-
-    @pl.when(ctx < 1)
-    def _():
-        for a in range(2):
-            window[a, pl.ds(rows, rows), :] = zero_block
-
-    @pl.when(ctx < 2)
-    def _():
-        for a in range(2):
-            window[a, pl.ds(0, rows), :] = zero_block
-
-    for dist in (1, 2):
-
-        @pl.when(ctx + dist >= n_ctx)
-        def _():
-            for a in range(2):
-                got[a, dist - 1] = zero_block
-
-    acc[...] = jnp.zeros_like(acc)
 
     def columns(of_head):
         return pl.ds(pl.multiple_of(of_head * HEAD_SIZE, HEAD_SIZE), HEAD_SIZE)
@@ -161,51 +129,6 @@
 
     def zone_rows(of_zone, base=0):
         return pl.ds(pl.multiple_of(base + of_zone * group_rows, group_rows), group_rows)
-
-    loads[0].wait()
-    loads[1].wait()
-    self_copies = []
-    for a in range(2):
-        copy = pltpu.make_async_copy(
-            stage.at[a, :, columns(head)],
-            window.at[a, piece_rows(head, SPAN * rows), :],
-            self_sem.at[a],
-        )
-        copy.start()
-        self_copies.append(copy)
-    loads[2].wait()
-
-    row_place = lax.broadcasted_iota(jnp.int32, (TILE, TILE), 0)
-    column_place = lax.broadcasted_iota(jnp.int32, (TILE, TILE), 1)
-    for i in range(2):
-        query_docs = jnp.broadcast_to(
-            doc[pl.ds(2 * ctx + i, 1), :].astype(F32), (TILE, TILE)
-        ).T
-        for j in range(5):
-            doc_row = 2 * ctx - 2 * SPAN + i + j
-            key_docs = doc[pl.ds(jnp.maximum(doc_row, 0), 1), :].astype(F32)
-            seen = query_docs == key_docs
-            if j == 4:
-                seen = seen & (column_place <= row_place)
-            outside = jnp.where(doc_row >= 0, 0.0, MASKED).astype(F32)
-            bias[i, :, pl.ds(j * TILE, TILE)] = jnp.where(seen, 0.0, MASKED) + outside
-
-    for copy in head_loads:
-        copy.wait()
-    for i in range(2):
-        for h in range(heads):
-            at = pl.ds(h * TILE, TILE)
-            qt[i, :, at] = qs[i, at, :].T
-            gt[i, :, at] = gs[i, at, :].T
-
-    pl.semaphore_wait(
-        barrier,
-        5
-        + has_later[0].astype(jnp.int32)
-        + has_later[1].astype(jnp.int32)
-        + has_earlier[0].astype(jnp.int32)
-        + has_earlier[1].astype(jnp.int32),
-    )
 
     sends = []
 
@@ -264,15 +187,34 @@
                 (ctx, after * 2 + core),
             )
 
-    for a in range(2):
-        source_of = lambda to_head: stage.at[a, :, columns(to_head)]
-        mine = window.at[a, piece_rows(head, SPAN * rows), :]
-        exchange_far(source_of, relay.at[a], fwd_send.at[a], fwd_relay_recv.at[a])
-        exchange_near(source_of, mine, plus, fwd_send.at[a], fwd_recv.at[a, head], 2)
-        exchange_near(source_of, mine, minus, fwd_send.at[a], fwd_recv.at[a, head], 4)
+    def stage_of(a):
+        return lambda to_head: stage.at[a, :, columns(to_head)]
+
+    def mine_of(a):
+        return window.at[a, piece_rows(head, SPAN * rows), :]
+
+    def start_far(a):
+        exchange_far(stage_of(a), relay.at[a], fwd_send.at[a], fwd_relay_recv.at[a])
+
+    def start_partner(a):
         send(
-            source_of(partner), mine, fwd_send.at[a, 6], fwd_recv.at[a, head], (ctx, partner)
+            stage_of(a)(partner),
+            mine_of(a),
+            fwd_send.at[a, 6],
+            fwd_recv.at[a, head],
+            (ctx, partner),
         )
+
+    def start_near(a):
+        for zone_number, slot in ((plus, 2), (minus, 4)):
+            exchange_near(
+                stage_of(a),
+                mine_of(a),
+                zone_number,
+                fwd_send.at[a],
+                fwd_recv.at[a, head],
+                slot,
+            )
 
     def window_piece(a, of_head):
         return window.at[a, piece_rows(of_head, SPAN * rows), :]
@@ -305,16 +247,99 @@
             lambda origin: fwd_recv.at[a, origin],
         )
 
+    loads[0].wait()
+    loads[1].wait()
+    self_copies = []
+    for a in range(2):
+        copy = pltpu.make_async_copy(
+            stage.at[a, :, columns(head)],
+            window.at[a, piece_rows(head, SPAN * rows), :],
+            self_sem.at[a],
+        )
+        copy.start()
+        self_copies.append(copy)
+
+    pl.semaphore_wait(
+        barrier,
+        5
+        + has_later[0].astype(jnp.int32)
+        + has_later[1].astype(jnp.int32)
+        + has_earlier[0].astype(jnp.int32)
+        + has_earlier[1].astype(jnp.int32),
+    )
+    start_far(0)
+
+    head_loads = []
+    for which, (source, target) in enumerate(((q_hbm, qs), (g_hbm, gs))):
+        for i in range(2):
+            for h in range(heads):
+                copy = pltpu.make_async_copy(
+                    source.at[pl.ds(i * TILE, TILE), pl.ds(h * TILE, TILE)],
+                    target.at[i, pl.ds(h * TILE, TILE), :],
+                    head_load_sem.at[which, i, h],
+                )
+                copy.start()
+                head_loads.append(copy)
+    loads[2].wait()
+
+    row_place = lax.broadcasted_iota(jnp.int32, (TILE, TILE), 0)
+    column_place = lax.broadcasted_iota(jnp.int32, (TILE, TILE), 1)
+    for i in range(2):
+        query_docs = jnp.broadcast_to(
+            doc[pl.ds(2 * ctx + i, 1), :].astype(F32), (TILE, TILE)
+        ).T
+        for j in range(5):
+            doc_row = 2 * ctx - 2 * SPAN + i + j
+            key_docs = doc[pl.ds(jnp.maximum(doc_row, 0), 1), :].astype(F32)
+            seen = query_docs == key_docs
+            if j == 4:
+                seen = seen & (column_place <= row_place)
+            outside = jnp.where(doc_row >= 0, 0.0, MASKED).astype(F32)
+            bias[i, :, pl.ds(j * TILE, TILE)] = jnp.where(seen, 0.0, MASKED) + outside
+
+    start_partner(0)
+    start_near(0)
+    start_partner(1)
     hand_on(0, 3)
+
+    for copy in head_loads:
+        copy.wait()
+    for i in range(2):
+        for h in range(heads):
+            at = pl.ds(h * TILE, TILE)
+            qt[i, :, at] = qs[i, at, :].T
+            gt[i, :, at] = gs[i, at, :].T
+
+    start_far(1)
     hand_on(1, 3)
+
+    zero_block = jnp.zeros((rows, HEAD_SIZE), BF16)
+
+    @pl.when(ctx < 1)
+    def _():
+        for a in range(2):
+            window[a, pl.ds(rows, rows), :] = zero_block
+
+    @pl.when(ctx < 2)
+    def _():
+        for a in range(2):
+            window[a, pl.ds(0, rows), :] = zero_block
+
+    for dist in (1, 2):
+
+        @pl.when(ctx + dist >= n_ctx)
+        def _():
+            for a in range(2):
+                got[a, dist - 1] = zero_block
+
+    acc[...] = jnp.zeros_like(acc)
+
     relay_forward(0)
+    start_near(1)
     hand_on(0, 1)
     hand_on(0, 2)
     relay_forward(1)
-    hand_on(1, 1)
-    hand_on(1, 2)
     hand_on(0, 0)
-    hand_on(1, 0)
 
     def window_here(a):
         for r in (3, 1, 2, 0):
@@ -327,30 +352,50 @@
                         ctx_recv.at[a, dist - 1, r],
                     )
 
-    blocks = heads // 2
+    blocks = heads // BLOCK_HEADS
+    block_rows = BLOCK_HEADS * TILE
 
     def block_of(n):
         i = n // blocks
-        at = pl.ds(pl.multiple_of(lax.rem(n, blocks) * (2 * TILE), 2 * TILE), 2 * TILE)
-        span = pl.ds(pl.multiple_of(i * TILE, TILE), reach)
-        return i, at, span
-
+        return i, pl.ds(n % blocks * block_rows, block_rows), pl.ds(i * TILE, reach)
+
+    def put_heads(out, n, block):
+        at_rows = pl.ds(n // blocks * TILE, TILE)
+        first = n % blocks * BLOCK_HEADS
+        for h in range(BLOCK_HEADS):
+            at_columns = pl.ds((first + h) * HEAD_SIZE, HEAD_SIZE)
+            out[at_rows, at_columns] = block[h * TILE : (h + 1) * TILE]
+
+    hand_on(1, 1)
+    hand_on(1, 2)
     window_here(0)
-
-    def probability_step(n, carry):
+    hand_on(1, 0)
+
+    every = reach // TILE
+
+    def score_stage(n):
         i, at, span = block_of(n)
+        mask = bias[i]
         scores = dot_nt(qs[i, at, :], window[0, span, :])
-        mask = bias[i]
-        scores = scores + jnp.concatenate([mask, mask], 0)
+        scores = scores + jnp.concatenate([mask] * BLOCK_HEADS, 0)
+        held[n % 2] = scores
         row_max = jnp.max(scores, axis=1, keepdims=True)
-        raised = jnp.exp2((scores - row_max) * EXP2_SCALE)
+        row_held[n % 2] = jnp.broadcast_to(row_max, (block_rows, TILE))
+
+    def probability_stage(n):
+        i, at, span = block_of(n)
+        row_max = jnp.concatenate([row_held[n % 2]] * every, 1)
+        raised = jnp.exp2((held[n % 2] - row_max) * EXP2_SCALE)
         inverse = 1.0 / jnp.sum(raised, axis=1, keepdims=True)
         probability = raised * inverse
         probs[i, at, :] = probability
         weights[i, at, :] = probability.astype(BF16)
-        return carry
-
-    lax.fori_loop(0, 2 * blocks, probability_step, 0)
+
+    score_stage(0)
+    for n in range(2 * blocks):
+        if n + 1 < 2 * blocks:
+            score_stage(n + 1)
+        probability_stage(n)
 
     def collect(g, left, right):
         for i in range(2):
@@ -377,36 +422,28 @@
 
     window_here(1)
 
-    def gradient_step(n, carry):
+    def output_stage(n):
         i, at, span = block_of(n)
-        value_window = window[1, span, :]
-        out_gradient = gs[i, at, :]
-        attended = dot_nn(weights[i, at, :], value_window).astype(BF16)
-        att_out[i, at, :] = attended
+        attended = dot_nn(weights[i, at, :], window[1, span, :]).astype(BF16)
+        put_heads(att_out, n, attended)
         delta = jnp.sum(
-            out_gradient.astype(F32) * attended.astype(F32), axis=1, keepdims=True
+            gs[i, at, :].astype(F32) * attended.astype(F32), axis=1, keepdims=True
         )
-        prob_grad = dot_nt(out_gradient, value_window)
+        row_held[n % 2] = jnp.broadcast_to(delta, (block_rows, TILE))
+
+    def gradient_stage(n):
+        i, at, span = block_of(n)
+        prob_grad = dot_nt(gs[i, at, :], window[1, span, :])
+        delta = jnp.concatenate([row_held[n % 2]] * every, 1)
         score_grad[i, at, :] = (probs[i, at, :] * (prob_grad - delta) * SCALE).astype(BF16)
-        return carry
-
-    lax.fori_loop(0, 2 * blocks, gradient_step, 0)
+
+    output_stage(0)
+    for n in range(2 * blocks):
+        if n + 1 < 2 * blocks:
+            output_stage(n + 1)
+        gradient_stage(n)
+
     collect(0, qt, score_grad)
-
-    outs = []
-
-    def write_out(which, source, target):
-        for i in range(2):
-            for h in range(heads):
-                copy = pltpu.make_async_copy(
-                    source.at[i, pl.ds(h * TILE, TILE), :],
-                    target.at[pl.ds(i * TILE, TILE), pl.ds(h * TILE, TILE)],
-                    out_sem.at[which, i, h],
-                )
-                copy.start()
-                outs.append(copy)
-
-    write_out(0, att_out, att_hbm)
 
     self_results = []
 
@@ -452,29 +489,24 @@
 
     send_home(1)
 
-    def query_step(n, carry):
+    for n in range(2 * blocks):
         i, at, span = block_of(n)
-        dq_out[i, at, :] = dot_nn(score_grad[i, at, :], window[0, span, :]).astype(BF16)
-        return carry
-
-    lax.fori_loop(0, 2 * blocks, query_step, 0)
-    write_out(1, dq_out, dq_hbm)
+        put_heads(dq_out, n, dot_nn(score_grad[i, at, :], window[0, span, :]).astype(BF16))
+
     send_home(0)
     relay_home(1)
     relay_home(0)
 
     for copy in self_results:
         copy.wait()
-    for g, target in ((1, dv_hbm), (0, dk_hbm)):
+    for g, target in ((1, dv_out), (0, dk_out)):
         for r in (3, 1, 2, 0):
             for source_core in range(2):
                 origin = relative[r] * 2 + (1 - core if r == 3 else source_core)
                 if r == 3 and source_core:
                     continue
                 arrived(result.at[g, :, columns(origin)], back_recv.at[g, origin])
-        copy = pltpu.make_async_copy(result.at[g], target, result_sem.at[g])
-        copy.start()
-        outs.append(copy)
+        target[...] = result[g]
     for copy, wanted in sends:
         if wanted is None:
             copy.wait_send()
@@ -483,9 +515,6 @@
             @pl.when(wanted)
             def _():
                 copy.wait_send()
-
-    for copy in outs:
-        copy.wait()
 
 
 def on_device(n_ctx, queries, keys, values, doc_ids, output_gradient):
@@ -496,10 +525,14 @@
     stacked = heads * TILE
     reach = SPAN * rows + TILE
     docs = doc_ids.reshape(-1, TILE)
+    in_hbm = [
+        pltpu.with_memory_space_constraint(x, pltpu.HBM)
+        for x in (queries, keys, values, docs, output_gradient)
+    ]
     vmem = pltpu.VMEM
     dma = pltpu.SemaphoreType.DMA
     any_space = pl.BlockSpec(memory_space=pl.ANY)
-    return pl.pallas_call(
+    results = pl.pallas_call(
         functools.partial(kernel, n_ctx),
         out_shape=(
             jax.ShapeDtypeStruct((rows, width), BF16),
@@ -507,8 +540,8 @@
             jax.ShapeDtypeStruct((piece, key_width), BF16),
             jax.ShapeDtypeStruct((piece, key_width), BF16),
         ),
-        in_specs=[any_space] * 5,
-        out_specs=(any_space,) * 4,
+        in_specs=[pl.BlockSpec(memory_space=pltpu.HBM)] * 5,
+        out_specs=(pl.BlockSpec(memory_space=pltpu.VMEM),) * 4,
         scratch_shapes=[
             vmem((2, piece, key_width), BF16),
             vmem((2, all_rows, HEAD_SIZE), BF16),
@@ -522,8 +555,8 @@
             vmem((2, stacked, reach), F32),
             vmem((2, stacked, reach), BF16),
             vmem((2, stacked, reach), BF16),
-            vmem((2, stacked, HEAD_SIZE), BF16),
-            vmem((2, stacked, HEAD_SIZE), BF16),
+            vmem((2, BLOCK_HEADS * TILE, reach), F32),
+            vmem((2, BLOCK_HEADS * TILE, TILE), F32),
             vmem((2, HEAD_SIZE, all_rows), F32),
             vmem((2, SPAN * rows, HEAD_SIZE), BF16),
             vmem((2, rows, HEAD_SIZE), F32),
@@ -534,8 +567,6 @@
             dma((3,)),
             dma((2, 2, heads)),
             dma((4,)),
-            dma((2, 2, heads)),
-            dma((2,)),
             dma((2, 9)),
             dma((2, 2 * GROUPS)),
             dma((2, 2)),
@@ -547,8 +578,35 @@
             dma((2, 2 * GROUPS)),
             dma((2, 2)),
         ],
-        compiler_params=pltpu.CompilerParams(collective_id=0, has_side_effects=True),
-    )(queries, keys, values, docs, output_gradient)
+        compiler_params=pltpu.CompilerParams(
+            collective_id=0, has_side_effects=True, vmem_limit_bytes=LIMIT
+        ),
+    )(*in_hbm)
+    return write_results(results)
+
+
+def write_kernel(*refs):
+    count = len(refs) // 2
+    sources, targets, sem = refs[:count], refs[count : 2 * count], refs[-1]
+    copies = [
+        pltpu.make_async_copy(source, target, sem.at[n])
+        for n, (source, target) in enumerate(zip(sources, targets))
+    ]
+    for copy in copies:
+        copy.start()
+    for copy in copies:
+        copy.wait()
+
+
+def write_results(results):
+    return pl.pallas_call(
+        write_kernel,
+        out_shape=tuple(jax.ShapeDtypeStruct(r.shape, r.dtype) for r in results),
+        in_specs=[pl.BlockSpec(memory_space=pltpu.VMEM)] * len(results),
+        out_specs=(pl.BlockSpec(memory_space=pl.ANY),) * len(results),
+        scratch_shapes=[pltpu.SemaphoreType.DMA((len(results),))],
+        compiler_params=pltpu.CompilerParams(vmem_limit_bytes=LIMIT),
+    )(*results)
 
 
 def solution(mesh):

time: 85.6 us -> 76.9 us (0.90)
  the two profiles are of different devices: /device:TPU:124 before, /device:TPU:33 now
where the time goes in v2:
time: 76.9 us; the launch traced here: 76.6 us
  Pallas kernels  75.9 us (99%)
    pallas_call x1, Pallas kernels, on_device(): pl.pallas_call(functools.partial(kernel, n_ctx), out_shape=(jax.ShapeDtyp...  74.9 us

profile of v2, /device:TPU:33, one launch (start us, length us, event | category | flops | bytes accessed | tf_op | source)
XLA Modules:
  0.0 76.6 jit_solution(6336290218728653978)
XLA Ops:
  0.6 74.9 %shard_map.84 = (bf16[256,1024]{1,0:T(8,128)(2,1)S(1)}, bf16[256,1024]{1,0:T(8,128)(2,1)S(1)}, bf16[32,1024]{1,0:T(8,128)(2,1)S(1)}, bf16[32,1024]{1,0:T(8,128)(2,1)S(1)}) custom-call(bf16[256,1024]{1,0:T(8,128)(2,1)} %q_hbm.1, bf16[32,1024]{1,0:T(8,128)(2,1)} %k_hbm.1, bf16[32,1024]{1,0:T(8,128)(2,1)} %v_hbm.1, s32[256,128]{1,0:T(8,128)} %bitcast.1, ...), custom_call_target="tpu_custom_call" | custom-call | tf_op jit(solution)/shard_map/pallas_call | solution.py:535
  75.6 1.0 %shard_map.85 = (bf16[256,1024]{1,0:T(8,128)(2,1)}, bf16[256,1024]{1,0:T(8,128)(2,1)}, bf16[32,1024]{1,0:T(8,128)(2,1)}, bf16[32,1024]{1,0:T(8,128)(2,1)}) custom-call(bf16[256,1024]{1,0:T(8,128)(2,1)S(1)} %get-tuple-element.8.refs_0_, bf16[256,1024]{1,0:T(8,128)(2,1)S(1)} %get-tuple-element.9.refs_1_, bf16[32,1024]{1,0:T(8,128)(2,1)S(1)} %get-tuple-element.10.refs_2_, ...), custom_call_target="tpu_custom_call" | custom-call | tf_op jit(solution)/shard_map/pallas_call | solution.py:602

commit v3 on v2

--- a/solution.py
+++ b/solution.py
@@ -447,10 +447,10 @@
 
     self_results = []
 
-    def send_home(g):
+    def send_home(g, zones):
         mine = result.at[g, :, columns(head)]
         source_of = lambda to_head: home.at[g, piece_rows(to_head), :]
-        for r in range(GROUPS):
+        for r in zones:
             at = zone_rows(relative[r])
             for dist in (1, 2):
 
@@ -487,13 +487,15 @@
             lambda origin: back_recv.at[g, origin],
         )
 
-    send_home(1)
+    send_home(1, (0,))
 
     for n in range(2 * blocks):
         i, at, span = block_of(n)
         put_heads(dq_out, n, dot_nn(score_grad[i, at, :], window[0, span, :]).astype(BF16))
 
-    send_home(0)
+    send_home(0, (0,))
+    send_home(1, (1, 2, 3))
+    send_home(0, (1, 2, 3))
     relay_home(1)
     relay_home(0)
 

time: 76.9 us -> 75.7 us (0.984)
  Pallas kernels: 75.9 us -> 74.8 us
    pallas_call x1, Pallas kernels: 74.9 us -> 73.8 us  [on_device(): pl.pallas_call(functools.partial(kernel, n_ctx), out_shape=(jax.ShapeDtyp...]
where the time goes in v3:
time: 75.7 us; the launch traced here: 75.4 us
  Pallas kernels  74.8 us (99%)
    pallas_call x1, Pallas kernels, on_device(): pl.pallas_call(functools.partial(kernel, n_ctx), out_shape=(jax.ShapeDtyp...  73.8 us

profile of v3, /device:TPU:33, one launch (start us, length us, event | category | flops | bytes accessed | tf_op | source)
XLA Modules:
  0.0 75.4 jit_solution(2996979541308618857)
XLA Ops:
  0.6 73.8 %shard_map.84 = (bf16[256,1024]{1,0:T(8,128)(2,1)S(1)}, bf16[256,1024]{1,0:T(8,128)(2,1)S(1)}, bf16[32,1024]{1,0:T(8,128)(2,1)S(1)}, bf16[32,1024]{1,0:T(8,128)(2,1)S(1)}) custom-call(bf16[256,1024]{1,0:T(8,128)(2,1)} %q_hbm.1, bf16[32,1024]{1,0:T(8,128)(2,1)} %k_hbm.1, bf16[32,1024]{1,0:T(8,128)(2,1)} %v_hbm.1, s32[256,128]{1,0:T(8,128)} %bitcast.1, ...), custom_call_target="tpu_custom_call" | custom-call | tf_op jit(solution)/shard_map/pallas_call | solution.py:537
  74.4 1.0 %shard_map.85 = (bf16[256,1024]{1,0:T(8,128)(2,1)}, bf16[256,1024]{1,0:T(8,128)(2,1)}, bf16[32,1024]{1,0:T(8,128)(2,1)}, bf16[32,1024]{1,0:T(8,128)(2,1)}) custom-call(bf16[256,1024]{1,0:T(8,128)(2,1)S(1)} %get-tuple-element.8.refs_0_, bf16[256,1024]{1,0:T(8,128)(2,1)S(1)} %get-tuple-element.9.refs_1_, bf16[32,1024]{1,0:T(8,128)(2,1)S(1)} %get-tuple-element.10.refs_2_, ...), custom_call_target="tpu_custom_call" | custom-call | tf_op jit(solution)/shard_map/pallas_call | solution.py:604
